TPU v7x, 128 devices: a whole 4x4x4 slice. The times are simulated.
128 devices in a mesh: row: 8 (over y, core), col: 16 (over x, z).
Axes of the slice: x: 4, y: 4, z: 4, core: 2. Of those that a mesh axis runs over, the one named last changes fastest.
Arguments:
- contribution: float32 [8, 8, 4, 16, 128, 128], P(None, 'row', None, 'col'), may hold values from -6 to 6
- parent_tiles: float32 [16, 8, 8, 16, 128, 128], P(None, 'row', None, 'col'), may hold values from -6 to 6
- row_basis: float32 [8, 8, 64, 128], P(None, 'row'), may hold values from -2.4 to 2.4
- pivot_basis: float32 [8, 8, 64, 2048], P(None, 'row', None, 'col'), may hold values from -0.125 to 0.125
- tile_ranks: int32 [64], replicated, may hold values from 16 to 64, as said below
- block_map: int32 [64], replicated, may hold values from 0 to 127, as said below
- panel_start: int32 [1], replicated, may hold values from 0 to 63
- pivot_inverse: float32 [512, 512], replicated
Outputs:
- updated_parent: float32 [16, 8, 8, 16, 128, 128], P(None, 'row', None, 'col')
Inputs may be any that keep to these rules, and one draw needn't show every extreme that they name: `tile_ranks`: multiples of 16; both 16 and 64 occur. `block_map`: child tile row u * 16 + l, for 0 <= l < 16, maps to parent tile row 2 * 16 * u + h_u + l with 0 <= h_u < 16; the 4 values h_u are distinct modulo 8.
All inputs are finite; a program needn't handle non-finite values.
Results may differ from a plain program's by a relative error of at most 0.0003.
Values sent between devices are 32-bit elements; how exact they have to be, the bound alone decides.
No kernel may reach another device: no remote copies, remote signals or barrier semaphores. Data moves between devices by JAX's collectives and lax.ppermute only.
A program may use at most 128 MiB of HBM per device.

v0:
```python
import jax
import jax.numpy as jnp
from jax import lax
from jax.sharding import PartitionSpec as P

PANEL_T = 4
highest = lax.Precision.HIGHEST


def spread_2(x, axis, root):
    mine = lax.axis_index(axis) == root
    return lax.psum(jnp.where(mine, x, jnp.zeros_like(x)), axis)


def from_behind(x, axis, by):
    count = lax.axis_size(axis)
    return lax.ppermute(x, axis, [(i, (i + by) % count) for i in range(count)])


def select_entries(lookup, wanted):
    matches = wanted[:, None] == jnp.arange(lookup.shape[0], dtype=jnp.int32)[None, :]
    return jnp.sum(jnp.where(matches, lookup[None, :], 0), axis=1)


def keep_ranks(factor, tile_index, rank_table):
    limits = select_entries(rank_table, tile_index)
    kept_cols = (jnp.arange(factor.shape[1], dtype=jnp.int32)[None, :] < limits[:, None]).astype(
        jnp.float32
    )
    return factor * kept_cols[:, :, None]


def every_other(stacked, groups, offset):
    shaped = stacked.reshape((groups, stacked.shape[0] // groups) + stacked.shape[1:])
    return lax.dynamic_index_in_dim(shaped, offset, axis=1, keepdims=False)


def per_device(
    contribution,
    parent_tiles,
    row_basis,
    pivot_basis,
    tile_ranks,
    block_map,
    panel_start,
    pivot_inverse,
):
    rows_grid = lax.axis_size("row")
    cols_grid = lax.axis_size("col")
    my_row = lax.axis_index("row")
    my_col = lax.axis_index("col")
    local_rows = contribution.shape[0]
    local_cols = contribution.shape[2]
    parent_rows = parent_tiles.shape[0]
    parent_cols = parent_tiles.shape[2]
    rank_max = row_basis.shape[2]
    per_block = cols_grid // rows_grid
    row_index = jnp.arange(local_rows, dtype=jnp.int32) * rows_grid + my_row
    col_index = jnp.arange(local_cols, dtype=jnp.int32) * cols_grid + my_col
    root_row = my_col % rows_grid
    offset = my_col // rows_grid
    own_basis = keep_ranks(row_basis[:, 0], row_index, tile_ranks)
    own_pivots = pivot_basis[:, 0]
    basis_picked = every_other(row_basis[:, 0], local_cols, offset)
    col_basis = spread_2(basis_picked, "row", root_row)
    all_pivots = lax.all_gather(pivot_basis, "row", axis=1, tiled=True)
    pivot_width = pivot_basis.shape[3]
    grouped = all_pivots.reshape(local_cols, cols_grid, rank_max, pivot_width)
    products = jnp.einsum(
        "trp,scup->cstru",
        own_pivots,
        grouped,
        precision=highest,
        preferred_element_type=jnp.float32,
    )
    weights = lax.psum_scatter(
        products.reshape(lax.axis_size("col") * local_cols, local_rows, rank_max * rank_max),
        "col",
        scatter_dimension=0,
        tiled=True,
    )
    weights = weights.reshape(local_cols, local_rows, rank_max, rank_max)
    col_basis = keep_ranks(col_basis, col_index, tile_ranks)
    half_product = jnp.einsum(
        "trx,stru->tsux", own_basis, weights, precision=highest, preferred_element_type=jnp.float32
    )
    update = jnp.einsum(
        "tsux,suy->tsxy",
        half_product,
        col_basis,
        precision=highest,
        preferred_element_type=jnp.float32,
    )
    lower_mask = (row_index[:, None] >= col_index[None, :])[:, :, None, None]
    payload = jnp.where(lower_mask, contribution[:, 0, :, 0] - update, jnp.float32(0.0))
    block_first = jnp.arange(local_cols, dtype=jnp.int32) * cols_grid
    shifts = select_entries(block_map, block_first) - 2 * block_first
    row_shift = jnp.repeat(shifts, per_block) % rows_grid
    for bit_index in range((rows_grid - 1).bit_length()):
        arrived = from_behind(payload, "row", 1 << bit_index)
        taken = row_shift // (1 << bit_index) % 2 == 1
        payload = jnp.where(taken[:, None, None, None], arrived, payload)
    for bit_index in range((cols_grid - 1).bit_length()):
        arrived = from_behind(payload, "col", 1 << bit_index)
        taken = shifts // (1 << bit_index) % 2 == 1
        payload = jnp.where(taken[None, :, None, None], arrived, payload)
    row_source = (my_row - row_shift) % rows_grid
    target_rows = (
        select_entries(block_map, jnp.arange(local_rows, dtype=jnp.int32) * rows_grid + row_source)
        // rows_grid
    )
    col_source = (my_col - shifts) % cols_grid
    target_cols = (
        select_entries(block_map, jnp.arange(local_cols, dtype=jnp.int32) * cols_grid + col_source)
        // cols_grid
    )
    row_place = (jnp.arange(parent_rows, dtype=jnp.int32)[:, None] == target_rows[None, :]).astype(
        jnp.float32
    )
    col_place = (jnp.arange(parent_cols, dtype=jnp.int32)[:, None] == target_cols[None, :]).astype(
        jnp.float32
    )
    spread = jnp.einsum(
        "at,tsxy->asxy", row_place, payload, precision=highest, preferred_element_type=jnp.float32
    )
    spread = jnp.einsum(
        "bs,asxy->abxy", col_place, spread, precision=highest, preferred_element_type=jnp.float32
    )
    assembled = parent_tiles[:, 0, :, 0] + spread
    start_col = panel_start[0]
    panel_parts = []
    for panel_index in range(PANEL_T):
        column_id = start_col + panel_index
        column = lax.dynamic_index_in_dim(assembled, column_id // cols_grid, axis=1, keepdims=False)
        panel_parts.append(spread_2(column, "col", column_id % cols_grid))
    row_panel = jnp.concatenate(panel_parts, axis=2)
    col_panel = spread_2(every_other(row_panel, parent_cols, offset), "row", root_row)
    scaled = jnp.einsum(
        "axp,pq->axq",
        row_panel,
        pivot_inverse,
        precision=highest,
        preferred_element_type=jnp.float32,
    )
    trailing = jnp.einsum(
        "axq,byq->abxy", scaled, col_panel, precision=highest, preferred_element_type=jnp.float32
    )
    big_rows = jnp.arange(parent_rows, dtype=jnp.int32) * rows_grid + my_row
    big_cols = jnp.arange(parent_cols, dtype=jnp.int32) * cols_grid + my_col
    window = (big_rows[:, None] >= big_cols[None, :]) & (big_cols[None, :] >= start_col + PANEL_T)
    result = jnp.where(window[:, :, None, None], assembled - trailing, assembled)
    return result[:, None, :, None]


def solution(mesh):
    placed = (
        P(None, "row", None, "col", None, None),
        P(None, "row", None, "col", None, None),
        P(None, "row", None, None),
        P(None, "row", None, "col"),
        P(),
        P(),
        P(),
        P(),
    )
    return jax.shard_map(
        per_device,
        mesh=mesh,
        in_specs=placed,
        out_specs=P(None, "row", None, "col", None, None),
        check_vma=False,
    )
```

profile of v0, /device:TPU:0, one launch (start us, length us, event | category | flops | bytes accessed | tf_op | source)
XLA Modules:
  0.0 810.4 jit_solution(2350074608308215927)
XLA Ops:
  6.5 0.7 all-gather.2.cloned.1.call-update
  7.3 29.4 %all-gather.2.cloned.1.call-done = f32[8,8,64,128]{3,2,1,0:T(8,128)} async-done(((f32[8,1,64,128]{3,2,1,0:T(8,128)}), f32[8,8,64,128]{3,2,1,0:T(8,128)}) %all-gather.2.cloned.1.call-update) | async-done | bytes 2097168 | tf_op jit(solution)/shard_map/all_gather | solution.py:66
  36.7 17.0 %convolution_bitcast_fusion = f32[16,4,8,64,64]{3,4,2,0,1:T(8,128)} fusion(f32[4,16,64,128,1]{3,2,4,1,0:T(8,128)} %bitcast.109, f32[8,1,64,128]{3,2,1,0:T(8,128)} %param.11), kind=kOutput, calls=%fused_computation.1 | convolution fusion | flops 3221225472 | bytes 10747904 | tf_op jit(solution)/shard_map/trp,scup->cstru/dot_general | solution.py:69
  53.7 17.6 %copy.33 = f32[16,4,8,64,64]{4,3,2,1,0:T(8,128)} copy(f32[16,4,8,64,64]{3,4,2,0,1:T(8,128)} %convolution_bitcast_fusion) | data formatting | bytes 16777216 | tf_op jit(solution)/shard_map/trp,scup->cstru/transpose | solution.py:69
  71.3 14.7 %reshape.468 = f32[64,8,4096]{2,1,0:T(8,128)} reshape(f32[16,4,8,64,64]{4,3,2,1,0:T(8,128)} %copy.33) | data formatting | bytes 16777216 | tf_op jit(solution)/shard_map/reshape | solution.py:77
  86.2 0.8 copy-done.7
  87.0 0.7 fusion.15
  87.8 0.1 broadcast_compare_fusion
  87.9 0.2 select_reduce_fusion.3
  88.1 0.2 select_reduce_fusion
  88.4 1.8 copy.31
  90.2 81.4 %reduce-scatter.2.cloned.1.call-done = f32[4,8,4096]{2,1,0:T(8,128)} async-done(((f32[64,8,4096]{2,1,0:T(8,128)}), f32[4,8,4096]{2,1,0:T(8,128)}) %reduce-scatter.2.cloned.1.call-update) | async-done | bytes 524304 | tf_op jit(solution)/shard_map/reduce_scatter | solution.py:76
  171.7 1.5 reshape.469
  173.1 2.9 fusion.13
  176.0 56.6 %all-reduce.5.cloned.1.call-done = f32[4,64,128]{2,1,0:T(8,128)} async-done(((f32[4,64,128]{2,1,0:T(8,128)}), f32[4,64,128]{2,1,0:T(8,128)}) %all-reduce.5.cloned.1.call-update) | async-done | bytes 131088 | tf_op jit(solution)/shard_map/psum | solution.py:12
  232.6 3.9 fusion.9
  236.6 0.2 select_reduce_fusion.4
  236.9 0.1 reshape.466
  237.0 26.3 %collective-permute-done = f32[8,4,128,128]{2,3,0,1:T(8,128)} collective-permute-done((f32[8,4,128,128]{2,3,0,1:T(8,128)S(1)}, f32[8,4,128,128]{2,3,0,1:T(8,128)}, u32[]{:S(2)}, u32[]{:S(2)}) %collective-permute-start) | collective-permute-done | bytes 2097184 | tf_op jit(solution)/shard_map/ppermute | solution.py:17
  263.4 1.9 broadcast_select_fusion.1
  265.3 0.1 collective-permute-start.1
  265.3 45.3 %collective-permute-done.1 = f32[8,4,128,128]{2,3,0,1:T(8,128)S(1)} collective-permute-done((f32[8,4,128,128]{2,3,0,1:T(8,128)S(1)}, f32[8,4,128,128]{2,3,0,1:T(8,128)S(1)}, u32[]{:S(2)}, u32[]{:S(2)}) %collective-permute-start.1) | collective-permute-done | bytes 2097184 | tf_op jit(solution)/shard_map/ppermute | solution.py:17
  310.7 0.4 broadcast_select_fusion.2
  311.1 0.8 collective-permute-start.2
  311.9 45.3 %collective-permute-done.2 = f32[8,4,128,128]{2,3,0,1:T(8,128)S(1)} collective-permute-done((f32[8,4,128,128]{2,3,0,1:T(8,128)S(1)}, f32[8,4,128,128]{2,3,0,1:T(8,128)S(1)}, u32[]{:S(2)}, u32[]{:S(2)}) %collective-permute-start.2) | collective-permute-done | bytes 2097184 | tf_op jit(solution)/shard_map/ppermute | solution.py:17
  357.2 0.4 broadcast_select_fusion.3
  357.6 2.1 collective-permute-start.3
  359.7 47.1 %collective-permute-done.3 = f32[8,4,128,128]{2,3,0,1:T(8,128)S(1)} collective-permute-done((f32[8,4,128,128]{2,3,0,1:T(8,128)S(1)}, f32[8,4,128,128]{2,3,0,1:T(8,128)S(1)}, u32[]{:S(2)}, u32[]{:S(2)}) %collective-permute-start.3) | collective-permute-done | bytes 2097184 | tf_op jit(solution)/shard_map/ppermute | solution.py:17
  406.8 0.4 broadcast_select_fusion.4
  407.2 0.1 collective-permute-start.4
  407.3 49.8 %collective-permute-done.4 = f32[8,4,128,128]{2,3,0,1:T(8,128)S(1)} collective-permute-done((f32[8,4,128,128]{2,3,0,1:T(8,128)S(1)}, f32[8,4,128,128]{2,3,0,1:T(8,128)S(1)}, u32[]{:S(2)}, u32[]{:S(2)}) %collective-permute-start.4) | collective-permute-done | bytes 2097184 | tf_op jit(solution)/shard_map/ppermute | solution.py:17
  457.1 0.4 broadcast_select_fusion.5
  457.5 0.1 collective-permute-start.5
  457.6 65.4 %collective-permute-done.5 = f32[8,4,128,128]{2,3,0,1:T(8,128)S(1)} collective-permute-done((f32[8,4,128,128]{2,3,0,1:T(8,128)S(1)}, f32[8,4,128,128]{2,3,0,1:T(8,128)S(1)}, u32[]{:S(2)}, u32[]{:S(2)}) %collective-permute-start.5) | collective-permute-done | bytes 2097184 | tf_op jit(solution)/shard_map/ppermute | solution.py:17
  522.9 0.3 broadcast_select_fusion.6
  523.3 0.1 collective-permute-start.6
  524.1 0.2 select_reduce_fusion.1
  524.3 0.2 select_reduce_fusion.2
  524.5 26.5 %collective-permute-done.6 = f32[8,4,128,128]{2,3,0,1:T(8,128)} collective-permute-done((f32[8,4,128,128]{2,3,0,1:T(8,128)S(1)}, f32[8,4,128,128]{2,3,0,1:T(8,128)}, u32[]{:S(2)}, u32[]{:S(2)}) %collective-permute-start.6) | collective-permute-done | bytes 2097184 | tf_op jit(solution)/shard_map/ppermute | solution.py:17
  551.0 3.2 broadcast_select_fusion.7
  554.2 2.0 copy.35
  556.3 1.9 fusion.21
  558.2 13.0 %bitcast_add_fusion = f32[16,8,128,128]{3,1,2,0:T(8,128)S(1)} fusion(f32[16,1,8,1,128,128]{5,4,3,2,1,0:T(8,128)} %param.9, f32[16,4,128,128]{3,0,2,1:T(8,128)S(1)} %fusion.21, s32[4]{0:T(128)S(1)} %and_select_fusion), kind=kOutput, calls=%fused_computation.3 | convolution fusion | flops 102760480 | bytes 20971536 | tf_op jit(solution)/shard_map/bs,asxy->abxy/dot_general | solution.py:126
  571.2 1.2 broadcast.768
  572.4 5.8 broadcast_select_fusion
  578.2 1.1 select_bitcast_fusion.2
  579.3 1.6 select_bitcast_fusion
  580.9 0.2 all-reduce.7.cloned.1.call-start
  581.1 104.7 %all-reduce.9.cloned.1.call-done = (f32[16,128,128]{2,1,0:T(8,128)}, f32[16,128,128]{2,1,0:T(8,128)}, f32[16,128,128]{2,1,0:T(8,128)}, f32[16,128,128]{2,1,0:T(8,128)}) async-done(((f32[16,128,128]{2,1,0:T(8,128)}, f32[16,128,128]{2,1,0:T(8,128)}, f32[16,128,128]{2,1,0:T(8,128)}, f32[16,128,128]{2,1,0:T(8,128)}), (f32[16,128,128]{2,1,0:T(8,128)}, f32[16,128,128]{2,1,0:T(8,128)}, f32[16,128,128]{2,1,0:T(8,128)}, ...) | async-done | bytes 4194320 | tf_op jit(solution)/shard_map/psum | solution.py:12
  685.8 1.5 constant_dynamic-update-slice_fusion.3
  687.4 0.1 constant_dynamic-update-slice_fusion.2
  687.5 0.2 copy-done.5
  687.7 0.1 constant_dynamic-update-slice_fusion.1
  687.8 0.9 copy-done.4
  688.7 0.1 constant_dynamic-update-slice_fusion
  688.8 1.9 copy-done.2
  690.8 1.6 fusion.7
  692.4 0.1 compare_and_fusion
  692.5 9.9 %fusion.10 = f32[16,128,512]{2,1,0:T(8,128)} fusion(f32[16,128,512]{2,1,0:T(8,128)} %copy-done.2, f32[512,512]{1,0:T(8,128)S(1)} %copy-done), kind=kOutput, calls=%fused_computation.14 | convolution fusion | flops 6442450944 | bytes 9437184 | tf_op jit(solution)/shard_map/axp,pq->axq/dot_general | solution.py:138
  702.4 55.5 %all-reduce.7.cloned.1.call-done = f32[8,128,512]{2,1,0:T(8,128)} async-done(((f32[8,128,512]{2,1,0:T(8,128)}), f32[8,128,512]{2,1,0:T(8,128)}) %all-reduce.7.cloned.1.call-update) | async-done | bytes 2097168 | tf_op jit(solution)/shard_map/psum | solution.py:12
  757.9 18.0 %fusion.1 = f32[8,128,16,128]{3,1,2,0:T(8,128)} fusion(f32[16,128,512]{2,1,0:T(8,128)} %fusion.10, f32[8,128,512]{2,1,0:T(8,128)} %all-reduce.7.cloned.1.call-done), kind=kOutput, calls=%fused_computation.4 | convolution fusion | flops 12884901888 | bytes 14680064 | tf_op jit(solution)/shard_map/axq,byq->abxy/dot_general | solution.py:145
  775.9 9.4 %copy.42 = f32[8,128,16,128]{1,0,3,2:T(8,128)} copy(f32[8,128,16,128]{3,1,2,0:T(8,128)} %fusion.1) | data formatting | bytes 16777216 | tf_op jit(solution)/shard_map/axq,byq->abxy/dot_general | solution.py:145
  785.3 10.2 %fusion = f32[16,1,8,1,128,128]{5,2,4,0,3,1:T(8,128)} fusion(f32[16,8,128,128]{3,1,2,0:T(8,128)} %copy-done.1, f32[8,128,16,128]{1,0,3,2:T(8,128)} %copy.42, pred[16,8]{1,0:T(8,128)(4,1)S(1)} %compare_and_fusion), kind=kLoop, calls=%fused_computation.2 | loop fusion | flops 4194304 | bytes 25165952 | tf_op jit(solution)/shard_map/broadcast_in_dim | solution.py:152
  795.4 8.2 %copy.43 = f32[16,1,8,1,128,128]{5,4,3,2,1,0:T(8,128)} copy(f32[16,1,8,1,128,128]{5,2,4,0,3,1:T(8,128)} %fusion) | data formatting | bytes 16777216 | tf_op jit(solution)/shard_map/broadcast_in_dim | solution.py:152
  (40 shorter events, 0.6 us)
Async XLA Ops:
  6.5 686.0 %copy-start = (f32[512,512]{1,0:T(8,128)S(1)}, f32[512,512]{1,0:T(8,128)}, u32[]{:S(2)}) copy-start(f32[512,512]{1,0:T(8,128)} %param.15) | copy-start | bytes 3145732
  6.5 30.2 %all-gather.2.cloned.1.call-start = ((), (), s32[]{:S(2)}) async-start(), calls=%async_computation.2 | async-start | bytes 2359296 | tf_op jit(solution)/shard_map/all_gather | solution.py:66
  7.3 164.4 %reduce-scatter.2.cloned.1.call-start = ((), (), s32[]{:S(2)}) async-start(), calls=%async_computation.3 | async-start | bytes 8912896 | tf_op jit(solution)/shard_map/reduce_scatter | solution.py:76
  86.1 0.9 copy-start.7
  86.1 1.8 copy-start.8
  86.1 2.3 copy-start.3
  86.1 146.5 %all-reduce.5.cloned.1.call-start = ((), (), s32[]{:S(2)}) async-start(), calls=%async_computation.1 | async-start | bytes 262144 | tf_op jit(solution)/shard_map/psum | solution.py:12
  87.7 598.1 %all-reduce.9.cloned.1.call-start = ((), (), s32[]{:S(2)}) async-start(), calls=%async_computation.5 | async-start | bytes 8388608 | tf_op jit(solution)/shard_map/psum | solution.py:12
  176.0 60.6 %copy-start.9 = (s32[64]{0:T(128)S(1)}, s32[64]{0:T(128)}, u32[]{:S(2)}) copy-start(s32[64]{0:T(128)} %param.13) | copy-start | bytes 772
  236.6 26.8 %collective-permute-start = (f32[8,4,128,128]{2,3,0,1:T(8,128)S(1)}, f32[8,4,128,128]{2,3,0,1:T(8,128)}, u32[]{:S(2)}, u32[]{:S(2)}) collective-permute-start(f32[8,4,128,128]{2,3,0,1:T(8,128)S(1)} %fusion.9), channel_id=1, source_target_pairs={{0,16},{16,32},{32,48},{48,64},{64,80},{80,96},{96,112},{112,0},{1... | collective-permute-start | bytes 6291464 | tf_op jit(solution)/shard_map/ppermute | solution.py:17
  265.3 45.4 %collective-permute-start.1 = (f32[8,4,128,128]{2,3,0,1:T(8,128)S(1)}, f32[8,4,128,128]{2,3,0,1:T(8,128)S(1)}, u32[]{:S(2)}, u32[]{:S(2)}) collective-permute-start(f32[8,4,128,128]{2,3,0,1:T(8,128)S(1)} %broadcast_select_fusion.1), channel_id=1, source_target_pairs={{0,32},{16,48},{32,64},{48,80},{64,96},{80,112},{96,0},{112,16},{1... | collective-permute-start | bytes 6291464 | tf_op jit(solution)/shard_map/ppermute | solution.py:17
  311.1 46.1 %collective-permute-start.2 = (f32[8,4,128,128]{2,3,0,1:T(8,128)S(1)}, f32[8,4,128,128]{2,3,0,1:T(8,128)S(1)}, u32[]{:S(2)}, u32[]{:S(2)}) collective-permute-start(f32[8,4,128,128]{2,3,0,1:T(8,128)S(1)} %broadcast_select_fusion.2), channel_id=1, source_target_pairs={{0,64},{16,80},{32,96},{48,112},{64,0},{80,16},{96,32},{112,48},{1... | collective-permute-start | bytes 6291464 | tf_op jit(solution)/shard_map/ppermute | solution.py:17
  357.6 49.2 %collective-permute-start.3 = (f32[8,4,128,128]{2,3,0,1:T(8,128)S(1)}, f32[8,4,128,128]{2,3,0,1:T(8,128)S(1)}, u32[]{:S(2)}, u32[]{:S(2)}) collective-permute-start(f32[8,4,128,128]{2,3,0,1:T(8,128)S(1)} %broadcast_select_fusion.3), channel_id=1, source_target_pairs={{0,1},{1,2},{2,3},{3,4},{4,5},{5,6},{6,7},{7,8},{8,9},{9,10},{10,1... | collective-permute-start | bytes 6291464 | tf_op jit(solution)/shard_map/ppermute | solution.py:17
  407.2 49.9 %collective-permute-start.4 = (f32[8,4,128,128]{2,3,0,1:T(8,128)S(1)}, f32[8,4,128,128]{2,3,0,1:T(8,128)S(1)}, u32[]{:S(2)}, u32[]{:S(2)}) collective-permute-start(f32[8,4,128,128]{2,3,0,1:T(8,128)S(1)} %broadcast_select_fusion.4), channel_id=1, source_target_pairs={{0,2},{1,3},{2,4},{3,5},{4,6},{5,7},{6,8},{7,9},{8,10},{9,11},{10,... | collective-permute-start | bytes 6291464 | tf_op jit(solution)/shard_map/ppermute | solution.py:17
  457.5 65.5 %collective-permute-start.5 = (f32[8,4,128,128]{2,3,0,1:T(8,128)S(1)}, f32[8,4,128,128]{2,3,0,1:T(8,128)S(1)}, u32[]{:S(2)}, u32[]{:S(2)}) collective-permute-start(f32[8,4,128,128]{2,3,0,1:T(8,128)S(1)} %broadcast_select_fusion.5), channel_id=1, source_target_pairs={{0,4},{1,5},{2,6},{3,7},{4,8},{5,9},{6,10},{7,11},{8,12},{9,13},{1... | collective-permute-start | bytes 6291464 | tf_op jit(solution)/shard_map/ppermute | solution.py:17
  523.3 27.7 %collective-permute-start.6 = (f32[8,4,128,128]{2,3,0,1:T(8,128)S(1)}, f32[8,4,128,128]{2,3,0,1:T(8,128)}, u32[]{:S(2)}, u32[]{:S(2)}) collective-permute-start(f32[8,4,128,128]{2,3,0,1:T(8,128)S(1)} %broadcast_select_fusion.6), channel_id=1, source_target_pairs={{0,8},{1,9},{2,10},{3,11},{4,12},{5,13},{6,14},{7,15},{8,0},{9,1},... | collective-permute-start | bytes 6291464 | tf_op jit(solution)/shard_map/ppermute | solution.py:17
  571.2 7.0 copy-start.1
  580.9 177.0 %all-reduce.7.cloned.1.call-start = ((), (), s32[]{:S(2)}) async-start(), calls=%async_computation.4 | async-start | bytes 4194304 | tf_op jit(solution)/shard_map/psum | solution.py:12
  685.8 1.5 copy-start.6
  685.8 1.9 copy-start.5
  687.4 1.3 copy-start.4
  688.8 2.0 copy-start.2
Sparse Core Ops, SparseCore 0:
  9.1 27.6 all-gather.1
  86.2 85.3 reduce-scatter.1
  174.0 58.6 all-reduce.4
  581.0 104.7 all-reduce.8
  692.5 65.3 all-reduce.6
where the time goes:
time: 820 us; the launch traced here: 810 us
  waiting for transfers between devices  634 us (77%)
  matrix products  66.6 us (8%)
  local copies, waits for them, and re-layouts  62.5 us (8%)
  other arithmetic  29.3 us (4%)
  between operations  14.4 us (2%)
    ppermute x7, waiting for transfers between devices, from_behind(): return lax.ppermute(x, axis, [(i, (i + by) % count) for i in range(count)])  306 us
    psum x3, waiting for transfers between devices, spread_2(): return lax.psum(jnp.where(mine, x, jnp.zeros_like(x)), axis)  217 us
    reduce_scatter x1, waiting for transfers between devices, per_device(): lax.psum_scatter(products.reshape(lax.axis_size('col') * local_cols, loca...  81.4 us
    all_gather x1, waiting for transfers between devices, per_device(): all_pivots = lax.all_gather(pivot_basis, 'row', axis=1, tiled=True)  29.4 us
    dot_general x1, matrix products, per_device(): jnp.einsum('axq,byq->abxy', scaled, col_panel, precision=highest, preferr...  18 us
    transpose x1, local copies, waits for them, and re-layouts, per_device(): jnp.einsum('trp,scup->cstru', own_pivots, grouped, precision=highest, pre...  17.6 us
    dot_general x1, matrix products, per_device(): jnp.einsum('trp,scup->cstru', own_pivots, grouped, precision=highest, pre...  17 us
  transfers between devices with their start and end apart: 12, of which 12 were waited for; matrix products, arithmetic and copies ran while one was open for 2% of the time, Pallas kernels for 0%

commit v1 on v0

--- a/solution.py
+++ b/solution.py
@@ -2,6 +2,7 @@
 import jax.numpy as jnp
 from jax import lax
 from jax.sharding import PartitionSpec as P
+from jax.lax import all_to_all, psum
 
 PANEL_T = 4
 highest = lax.Precision.HIGHEST
@@ -63,7 +64,11 @@
     own_pivots = pivot_basis[:, 0]
     basis_picked = every_other(row_basis[:, 0], local_cols, offset)
     col_basis = spread_2(basis_picked, "row", root_row)
-    all_pivots = lax.all_gather(pivot_basis, "row", axis=1, tiled=True)
+    total_devices = psum(1, "row")
+    parts_seen = [total_devices if at == 1 else 1 for at in range(pivot_basis.ndim)]
+    all_pivots = all_to_all(
+        jnp.tile(pivot_basis, parts_seen), "row", concat_axis=1, tiled=True, split_axis=1
+    )
     pivot_width = pivot_basis.shape[3]
     grouped = all_pivots.reshape(local_cols, cols_grid, rank_max, pivot_width)
     products = jnp.einsum(

time: 820 us -> 762 us (0.929)
  waiting for transfers between devices: 634 us -> 541 us
  blocking collectives: 0 us -> 31.9 us
    psum x3, waiting for transfers between devices: 217 us -> 160 us  [spread_2(): return lax.psum(jnp.where(mine, x, jnp.zeros_like(x)), axis)]
    all_to_all x0 -> x1, blocking collectives: none -> 31.9 us  [per_device(): all_to_all(jnp.tile(pivot_basis, parts_seen), 'row', concat_axis=1, tiled...]
    all_gather x1 -> x0, waiting for transfers between devices: 29.4 us -> none  [per_device(): all_pivots = lax.all_gather(pivot_basis, 'row', axis=1, tiled=True)]
  transfers between devices with their start and end apart: 12 -> 11, of which waited for: 12 -> 10; matrix products, arithmetic and copies ran while one was open for 2% -> 2% of each run, Pallas kernels for 0% -> 0%
where the time goes in v1:
time: 762 us; the launch traced here: 752 us
  waiting for transfers between devices  541 us (71%)
  matrix products  65.4 us (9%)
  local copies, waits for them, and re-layouts  64.7 us (8%)
  blocking collectives  31.9 us (4%)
  other arithmetic  29.2 us (4%)
  between operations  16.2 us (2%)
    ppermute x7, waiting for transfers between devices, from_behind(): return lax.ppermute(x, axis, [(i, (i + by) % count) for i in range(count)])  299 us
    psum x3, waiting for transfers between devices, spread_2(): return lax.psum(jnp.where(mine, x, jnp.zeros_like(x)), axis)  160 us
    reduce_scatter x1, waiting for transfers between devices, per_device(): lax.psum_scatter(products.reshape(lax.axis_size('col') * local_cols, loca...  81.4 us
    all_to_all x1, blocking collectives, per_device(): all_to_all(jnp.tile(pivot_basis, parts_seen), 'row', concat_axis=1, tiled...  31.9 us
    dot_general x1, matrix products, per_device(): jnp.einsum('axq,byq->abxy', scaled, col_panel, precision=highest, preferr...  18 us
    transpose x1, local copies, waits for them, and re-layouts, per_device(): jnp.einsum('trp,scup->cstru', own_pivots, grouped, precision=highest, pre...  17.6 us
    dot_general x1, matrix products, per_device(): jnp.einsum('trp,scup->cstru', own_pivots, grouped, precision=highest, pre...  15.9 us
  transfers between devices with their start and end apart: 11, of which 10 were waited for; matrix products, arithmetic and copies ran while one was open for 2% of the time, Pallas kernels for 0%

profile of v1, /device:TPU:0, one launch (start us, length us, event | category | flops | bytes accessed | tf_op | source)
XLA Modules:
  0.0 752.4 jit_solution(18433498306031218819)
XLA Ops:
  7.4 1.3 tile.10
  8.7 31.9 %all_to_all.5 = f32[8,8,64,128]{3,2,0,1:T(8,128)S(1)} all-to-all(f32[8,8,64,128]{3,2,0,1:T(8,128)S(1)} %tile.10), channel_id=1, replica_groups=mesh['row'=8,'col'=16] {'row'}, dimensions={1} | all-to-all | bytes 4194304 | tf_op jit(solution)/shard_map/all_to_all | solution.py:69
  40.5 0.2 copy.48
  40.8 0.7 copy-done.4
  41.5 15.9 %convolution_bitcast_fusion = f32[16,4,8,64,64]{3,4,2,0,1:T(8,128)} fusion(f32[4,16,64,128,1]{3,2,4,1,0:T(8,128)S(1)} %bitcast.104, f32[8,1,64,128]{3,2,1,0:T(8,128)S(1)} %copy-done.4), kind=kOutput, calls=%fused_computation.1 | convolution fusion | flops 3221225472 | bytes 10747904 | tf_op jit(solution)/shard_map/trp,scup->cstru/dot_general | solution.py:74
  57.3 17.6 %copy.49 = f32[16,4,8,64,64]{4,3,2,1,0:T(8,128)} copy(f32[16,4,8,64,64]{3,4,2,0,1:T(8,128)} %convolution_bitcast_fusion) | data formatting | bytes 16777216 | tf_op jit(solution)/shard_map/trp,scup->cstru/transpose | solution.py:74
  75.0 14.7 %reshape.471 = f32[64,8,4096]{2,1,0:T(8,128)} reshape(f32[16,4,8,64,64]{4,3,2,1,0:T(8,128)} %copy.49) | data formatting | bytes 16777216 | tf_op jit(solution)/shard_map/reshape | solution.py:82
  89.8 0.8 copy-done.8
  90.7 0.7 fusion.15
  91.5 0.2 select_reduce_fusion.3
  91.7 0.2 select_reduce_fusion
  92.0 1.8 copy.46
  93.8 81.4 %reduce-scatter.2.cloned.1.call-done = f32[4,8,4096]{2,1,0:T(8,128)} async-done(((f32[64,8,4096]{2,1,0:T(8,128)}), f32[4,8,4096]{2,1,0:T(8,128)}) %reduce-scatter.2.cloned.1.call-update) | async-done | bytes 524304 | tf_op jit(solution)/shard_map/reduce_scatter | solution.py:81
  175.3 1.5 reshape.472
  176.7 2.9 fusion.13
  179.6 3.9 fusion.9
  183.6 0.2 select_reduce_fusion.4
  183.9 0.1 reshape.469
  184.0 26.3 %collective-permute-done = f32[8,4,128,128]{2,3,0,1:T(8,128)} collective-permute-done((f32[8,4,128,128]{2,3,0,1:T(8,128)S(1)}, f32[8,4,128,128]{2,3,0,1:T(8,128)}, u32[]{:S(2)}, u32[]{:S(2)}) %collective-permute-start) | collective-permute-done | bytes 2097184 | tf_op jit(solution)/shard_map/ppermute | solution.py:18
  210.3 1.9 broadcast_select_fusion.1
  212.3 0.3 collective-permute-start.1
  212.6 46.3 %collective-permute-done.1 = f32[8,4,128,128]{2,3,0,1:T(8,128)S(1)} collective-permute-done((f32[8,4,128,128]{2,3,0,1:T(8,128)S(1)}, f32[8,4,128,128]{2,3,0,1:T(8,128)S(1)}, u32[]{:S(2)}, u32[]{:S(2)}) %collective-permute-start.1) | collective-permute-done | bytes 2097184 | tf_op jit(solution)/shard_map/ppermute | solution.py:18
  258.9 0.4 broadcast_select_fusion.2
  259.3 1.6 collective-permute-start.2
  260.9 44.4 %collective-permute-done.2 = f32[8,4,128,128]{2,3,0,1:T(8,128)S(1)} collective-permute-done((f32[8,4,128,128]{2,3,0,1:T(8,128)S(1)}, f32[8,4,128,128]{2,3,0,1:T(8,128)S(1)}, u32[]{:S(2)}, u32[]{:S(2)}) %collective-permute-start.2) | collective-permute-done | bytes 2097184 | tf_op jit(solution)/shard_map/ppermute | solution.py:18
  305.3 0.4 broadcast_select_fusion.3
  305.7 1.9 collective-permute-start.3
  307.7 46.5 %collective-permute-done.3 = f32[8,4,128,128]{2,3,0,1:T(8,128)S(1)} collective-permute-done((f32[8,4,128,128]{2,3,0,1:T(8,128)S(1)}, f32[8,4,128,128]{2,3,0,1:T(8,128)S(1)}, u32[]{:S(2)}, u32[]{:S(2)}) %collective-permute-start.3) | collective-permute-done | bytes 2097184 | tf_op jit(solution)/shard_map/ppermute | solution.py:18
  354.1 0.4 broadcast_select_fusion.4
  354.5 0.1 collective-permute-start.4
  354.6 49.8 %collective-permute-done.4 = f32[8,4,128,128]{2,3,0,1:T(8,128)S(1)} collective-permute-done((f32[8,4,128,128]{2,3,0,1:T(8,128)S(1)}, f32[8,4,128,128]{2,3,0,1:T(8,128)S(1)}, u32[]{:S(2)}, u32[]{:S(2)}) %collective-permute-start.4) | collective-permute-done | bytes 2097184 | tf_op jit(solution)/shard_map/ppermute | solution.py:18
  404.4 0.4 broadcast_select_fusion.5
  404.8 0.1 collective-permute-start.5
  404.9 59.5 %collective-permute-done.5 = f32[8,4,128,128]{2,3,0,1:T(8,128)S(1)} collective-permute-done((f32[8,4,128,128]{2,3,0,1:T(8,128)S(1)}, f32[8,4,128,128]{2,3,0,1:T(8,128)S(1)}, u32[]{:S(2)}, u32[]{:S(2)}) %collective-permute-start.5) | collective-permute-done | bytes 2097184 | tf_op jit(solution)/shard_map/ppermute | solution.py:18
  464.4 0.3 broadcast_select_fusion.6
  464.8 0.1 collective-permute-start.6
  465.6 0.2 select_reduce_fusion.1
  465.8 0.2 select_reduce_fusion.2
  466.0 26.5 %collective-permute-done.6 = f32[8,4,128,128]{2,3,0,1:T(8,128)} collective-permute-done((f32[8,4,128,128]{2,3,0,1:T(8,128)S(1)}, f32[8,4,128,128]{2,3,0,1:T(8,128)}, u32[]{:S(2)}, u32[]{:S(2)}) %collective-permute-start.6) | collective-permute-done | bytes 2097184 | tf_op jit(solution)/shard_map/ppermute | solution.py:18
  492.5 3.2 broadcast_select_fusion.7
  495.7 2.0 copy.51
  497.8 1.9 fusion.21
  499.7 13.0 %bitcast_add_fusion = f32[16,8,128,128]{3,1,2,0:T(8,128)S(1)} fusion(f32[16,1,8,1,128,128]{5,4,3,2,1,0:T(8,128)} %param.9, f32[16,4,128,128]{3,0,2,1:T(8,128)S(1)} %fusion.21, s32[4]{0:T(128)S(1)} %and_select_fusion), kind=kOutput, calls=%fused_computation.3 | convolution fusion | flops 102760480 | bytes 20971536 | tf_op jit(solution)/shard_map/bs,asxy->abxy/dot_general | solution.py:131
  512.7 1.2 broadcast.770
  513.9 5.8 broadcast_select_fusion
  519.7 1.1 select_bitcast_fusion.2
  520.8 1.6 select_bitcast_fusion
  522.4 0.2 all-reduce.7.cloned.1.call-start
  522.6 104.6 %all-reduce.9.cloned.1.call-done = (f32[16,128,128]{2,1,0:T(8,128)}, f32[16,128,128]{2,1,0:T(8,128)}, f32[16,128,128]{2,1,0:T(8,128)}, f32[16,128,128]{2,1,0:T(8,128)}) async-done(((f32[16,128,128]{2,1,0:T(8,128)}, f32[16,128,128]{2,1,0:T(8,128)}, f32[16,128,128]{2,1,0:T(8,128)}, f32[16,128,128]{2,1,0:T(8,128)}), (f32[16,128,128]{2,1,0:T(8,128)}, f32[16,128,128]{2,1,0:T(8,128)}, f32[16,128,128]{2,1,0:T(8,128)}, ...) | async-done | bytes 4194320 | tf_op jit(solution)/shard_map/psum | solution.py:13
  627.2 1.5 constant_dynamic-update-slice_fusion.3
  628.8 0.1 constant_dynamic-update-slice_fusion.2
  628.9 0.2 copy-done.6
  629.1 0.1 constant_dynamic-update-slice_fusion.1
  629.2 0.9 copy-done.5
  630.1 0.1 constant_dynamic-update-slice_fusion
  630.2 2.0 copy-done.2
  632.2 1.6 fusion.7
  633.8 0.1 compare_and_fusion
  633.9 9.8 %fusion.10 = f32[16,128,512]{2,1,0:T(8,128)} fusion(f32[16,128,512]{2,1,0:T(8,128)} %copy-done.2, f32[512,512]{1,0:T(8,128)S(1)} %copy-done), kind=kOutput, calls=%fused_computation.14 | convolution fusion | flops 6442450944 | bytes 9437184 | tf_op jit(solution)/shard_map/axp,pq->axq/dot_general | solution.py:143
  643.7 55.2 %all-reduce.7.cloned.1.call-done = f32[8,128,512]{2,1,0:T(8,128)} async-done(((f32[8,128,512]{2,1,0:T(8,128)}), f32[8,128,512]{2,1,0:T(8,128)}) %all-reduce.7.cloned.1.call-update) | async-done | bytes 2097168 | tf_op jit(solution)/shard_map/psum | solution.py:13
  698.9 18.0 %fusion.1 = f32[8,128,16,128]{3,1,2,0:T(8,128)} fusion(f32[16,128,512]{2,1,0:T(8,128)} %fusion.10, f32[8,128,512]{2,1,0:T(8,128)} %all-reduce.7.cloned.1.call-done), kind=kOutput, calls=%fused_computation.4 | convolution fusion | flops 12884901888 | bytes 14680064 | tf_op jit(solution)/shard_map/axq,byq->abxy/dot_general | solution.py:150
  716.9 9.4 %copy.58 = f32[8,128,16,128]{1,0,3,2:T(8,128)} copy(f32[8,128,16,128]{3,1,2,0:T(8,128)} %fusion.1) | data formatting | bytes 16777216 | tf_op jit(solution)/shard_map/axq,byq->abxy/dot_general | solution.py:150
  726.4 10.2 %fusion = f32[16,1,8,1,128,128]{5,2,4,0,3,1:T(8,128)} fusion(f32[16,8,128,128]{3,1,2,0:T(8,128)} %copy-done.1, f32[8,128,16,128]{1,0,3,2:T(8,128)} %copy.58, pred[16,8]{1,0:T(8,128)(4,1)S(1)} %compare_and_fusion), kind=kLoop, calls=%fused_computation.2 | loop fusion | flops 4194304 | bytes 25165952 | tf_op jit(solution)/shard_map/broadcast_in_dim | solution.py:157
  736.5 8.2 %copy.59 = f32[16,1,8,1,128,128]{5,4,3,2,1,0:T(8,128)} copy(f32[16,1,8,1,128,128]{5,2,4,0,3,1:T(8,128)} %fusion) | data formatting | bytes 16777216 | tf_op jit(solution)/shard_map/broadcast_in_dim | solution.py:157
  (42 shorter events, 0.7 us)
Async XLA Ops:
  7.4 626.5 %copy-start = (f32[512,512]{1,0:T(8,128)S(1)}, f32[512,512]{1,0:T(8,128)}, u32[]{:S(2)}) copy-start(f32[512,512]{1,0:T(8,128)} %param.15) | copy-start | bytes 3145732
  7.4 167.9 %reduce-scatter.2.cloned.1.call-start = ((), (), s32[]{:S(2)}) async-start(), calls=%async_computation.3 | async-start | bytes 8912896 | tf_op jit(solution)/shard_map/reduce_scatter | solution.py:81
  40.5 1.0 copy-start.4
  89.7 0.9 copy-start.8
  89.7 1.8 copy-start.9
  89.7 2.3 copy-start.3
  89.7 89.9 %all-reduce.5.cloned.1.call-start = ((), (), s32[]{:S(2)}) async-start(), calls=%async_computation.2 | async-start | bytes 262144 | tf_op jit(solution)/shard_map/psum | solution.py:13
  91.4 535.9 %all-reduce.9.cloned.1.call-start = ((), (), s32[]{:S(2)}) async-start(), calls=%async_computation.5 | async-start | bytes 8388608 | tf_op jit(solution)/shard_map/psum | solution.py:13
  179.6 4.0 copy-start.10
  183.6 26.8 %collective-permute-start = (f32[8,4,128,128]{2,3,0,1:T(8,128)S(1)}, f32[8,4,128,128]{2,3,0,1:T(8,128)}, u32[]{:S(2)}, u32[]{:S(2)}) collective-permute-start(f32[8,4,128,128]{2,3,0,1:T(8,128)S(1)} %fusion.9), channel_id=1, source_target_pairs={{0,16},{16,32},{32,48},{48,64},{64,80},{80,96},{96,112},{112,0},{1... | collective-permute-start | bytes 6291464 | tf_op jit(solution)/shard_map/ppermute | solution.py:18
  212.3 46.6 %collective-permute-start.1 = (f32[8,4,128,128]{2,3,0,1:T(8,128)S(1)}, f32[8,4,128,128]{2,3,0,1:T(8,128)S(1)}, u32[]{:S(2)}, u32[]{:S(2)}) collective-permute-start(f32[8,4,128,128]{2,3,0,1:T(8,128)S(1)} %broadcast_select_fusion.1), channel_id=1, source_target_pairs={{0,32},{16,48},{32,64},{48,80},{64,96},{80,112},{96,0},{112,16},{1... | collective-permute-start | bytes 6291464 | tf_op jit(solution)/shard_map/ppermute | solution.py:18
  259.3 46.0 %collective-permute-start.2 = (f32[8,4,128,128]{2,3,0,1:T(8,128)S(1)}, f32[8,4,128,128]{2,3,0,1:T(8,128)S(1)}, u32[]{:S(2)}, u32[]{:S(2)}) collective-permute-start(f32[8,4,128,128]{2,3,0,1:T(8,128)S(1)} %broadcast_select_fusion.2), channel_id=1, source_target_pairs={{0,64},{16,80},{32,96},{48,112},{64,0},{80,16},{96,32},{112,48},{1... | collective-permute-start | bytes 6291464 | tf_op jit(solution)/shard_map/ppermute | solution.py:18
  305.7 48.4 %collective-permute-start.3 = (f32[8,4,128,128]{2,3,0,1:T(8,128)S(1)}, f32[8,4,128,128]{2,3,0,1:T(8,128)S(1)}, u32[]{:S(2)}, u32[]{:S(2)}) collective-permute-start(f32[8,4,128,128]{2,3,0,1:T(8,128)S(1)} %broadcast_select_fusion.3), channel_id=1, source_target_pairs={{0,1},{1,2},{2,3},{3,4},{4,5},{5,6},{6,7},{7,8},{8,9},{9,10},{10,1... | collective-permute-start | bytes 6291464 | tf_op jit(solution)/shard_map/ppermute | solution.py:18
  354.5 49.9 %collective-permute-start.4 = (f32[8,4,128,128]{2,3,0,1:T(8,128)S(1)}, f32[8,4,128,128]{2,3,0,1:T(8,128)S(1)}, u32[]{:S(2)}, u32[]{:S(2)}) collective-permute-start(f32[8,4,128,128]{2,3,0,1:T(8,128)S(1)} %broadcast_select_fusion.4), channel_id=1, source_target_pairs={{0,2},{1,3},{2,4},{3,5},{4,6},{5,7},{6,8},{7,9},{8,10},{9,11},{10,... | collective-permute-start | bytes 6291464 | tf_op jit(solution)/shard_map/ppermute | solution.py:18
  404.8 59.6 %collective-permute-start.5 = (f32[8,4,128,128]{2,3,0,1:T(8,128)S(1)}, f32[8,4,128,128]{2,3,0,1:T(8,128)S(1)}, u32[]{:S(2)}, u32[]{:S(2)}) collective-permute-start(f32[8,4,128,128]{2,3,0,1:T(8,128)S(1)} %broadcast_select_fusion.5), channel_id=1, source_target_pairs={{0,4},{1,5},{2,6},{3,7},{4,8},{5,9},{6,10},{7,11},{8,12},{9,13},{1... | collective-permute-start | bytes 6291464 | tf_op jit(solution)/shard_map/ppermute | solution.py:18
  464.8 27.7 %collective-permute-start.6 = (f32[8,4,128,128]{2,3,0,1:T(8,128)S(1)}, f32[8,4,128,128]{2,3,0,1:T(8,128)}, u32[]{:S(2)}, u32[]{:S(2)}) collective-permute-start(f32[8,4,128,128]{2,3,0,1:T(8,128)S(1)} %broadcast_select_fusion.6), channel_id=1, source_target_pairs={{0,8},{1,9},{2,10},{3,11},{4,12},{5,13},{6,14},{7,15},{8,0},{9,1},... | collective-permute-start | bytes 6291464 | tf_op jit(solution)/shard_map/ppermute | solution.py:18
  512.7 7.0 copy-start.1
  522.4 176.6 %all-reduce.7.cloned.1.call-start = ((), (), s32[]{:S(2)}) async-start(), calls=%async_computation.4 | async-start | bytes 4194304 | tf_op jit(solution)/shard_map/psum | solution.py:13
  627.2 1.5 copy-start.7
  627.2 1.9 copy-start.6
  628.8 1.3 copy-start.5
  630.2 2.0 copy-start.2
Sparse Core Ops, SparseCore 0:
  89.9 85.3 reduce-scatter.1
  522.5 104.6 all-reduce.8
Sparse Core Ops, SparseCore 1:
  92.5 60.8 all-reduce.4
  633.9 65.0 all-reduce.6
